TPU v7x, 128 devices: a whole 4x4x4 slice. The times are simulated.
128 devices in a mesh: replica: 4 (over z), shard: 16 (over y, x_lo, core), tensor: 2 (over x_hi).
Axes of the slice: x: 4 (x_hi: 2, x_lo: 2; x = x_hi * 2 + x_lo), y: 4, z: 4, core: 2. Of those that a mesh axis runs over, the one named last changes fastest.
Arguments:
- trained_up: bfloat16 [4, 1024, 4096], P('replica', None, 'tensor'), may hold values from -6 to 6
- trained_down: bfloat16 [4, 4096, 1024], P('replica', 'tensor'), may hold values from -6 to 6
- trained_embed: bfloat16 [4, 32768, 1024], P('replica', ('shard', 'tensor')), may hold values from -6 to 6
- trained_norm: bfloat16 [4, 2, 1024], P('replica'), may hold values from 0.099609375 to 1.8984375
- master_up: float32 [1024, 4096], P(('replica', 'shard', 'tensor')), may hold values from -6 to 6
- moment_up: float32 [1024, 4096], P(('replica', 'shard', 'tensor')), may hold values from -4 to 4
- master_down: float32 [2, 2048, 1024], P('tensor', ('replica', 'shard')), may hold values from -6 to 6
- moment_down: float32 [2, 2048, 1024], P('tensor', ('replica', 'shard')), may hold values from -4 to 4
- master_embed: float32 [32, 1024, 1024], P(('shard', 'tensor'), 'replica'), may hold values from -6 to 6
- moment_embed: float32 [32, 1024, 64], P(('shard', 'tensor'), 'replica'), may hold values from -4 to 4
- master_norm: float32 [2, 1024], replicated, may hold values from 0.1 to 1.9
- moment_norm: float32 [2, 1024], replicated, may hold values from -2 to 2
- embed_basis: float32 [1024, 64], replicated, may hold values from -0.1875 to 0.1875
Outputs:
- recast_up: bfloat16 [1024, 4096], P(None, 'tensor')
- recast_down: bfloat16 [4096, 1024], P('tensor')
- recast_embed: bfloat16 [32768, 1024], P(('shard', 'tensor'))
- recast_norm: bfloat16 [2, 1024], replicated
- stored_up: float32 [1024, 4096], P(('replica', 'shard', 'tensor'))
- velocity_up: float32 [1024, 4096], P(('replica', 'shard', 'tensor'))
- stored_down: float32 [2, 2048, 1024], P('tensor', ('replica', 'shard'))
- velocity_down: float32 [2, 2048, 1024], P('tensor', ('replica', 'shard'))
- stored_embed: float32 [32, 1024, 1024], P(('shard', 'tensor'), 'replica')
- velocity_embed: float32 [32, 1024, 64], P(('shard', 'tensor'), 'replica')
- stored_norm: float32 [2, 1024], replicated
- velocity_norm: float32 [2, 1024], replicated
All inputs are finite; a program needn't handle non-finite values.
Results may differ from a plain program's by a relative error of at most 0.012.
Values may be sent and summed in bfloat16 or wider, within the bound.
A program may use at most 128 MiB of HBM per device.

v0:
```python
import jax
import jax.numpy as jnp
from jax import lax
from jax.sharding import PartitionSpec as P


def outer_step(master, moment, summed, groups):
    difference = master - summed / groups
    velocity = 0.5 * moment + difference
    return (master - 0.7 * (difference + 0.5 * velocity), velocity)


def body(
    trained_up,
    trained_down,
    trained_embed,
    trained_norm,
    master_up,
    moment_up,
    master_down,
    moment_down,
    master_embed,
    moment_embed,
    master_norm,
    moment_norm,
    embed_basis,
):
    replicas = lax.axis_size("replica")
    shards = lax.axis_size("shard")
    tensors = lax.axis_size("tensor")
    shard_pos = lax.axis_index("shard")
    width = embed_basis.shape[0]
    rows_up = master_up.shape[0]
    half_cols = trained_up.shape[2]
    rows_down = master_down.shape[1]
    up_blocks = trained_up[0].reshape(replicas, shards, tensors, rows_up, half_cols)
    up_own = lax.dynamic_index_in_dim(up_blocks, shard_pos, 1, keepdims=False)
    down_blocks = trained_down[0].reshape(replicas, shards, rows_down, width)
    down_own = lax.dynamic_index_in_dim(down_blocks, shard_pos, 1, keepdims=False)
    up_summed, down_summed = (
        lax.psum_scatter(
            up_own.astype(jnp.float32).astype(jnp.bfloat16),
            "replica",
            scatter_dimension=0,
            tiled=True,
        ).astype(jnp.float32),
        lax.psum_scatter(
            down_own.astype(jnp.float32).astype(jnp.bfloat16),
            "replica",
            scatter_dimension=0,
            tiled=True,
        ).astype(jnp.float32),
    )
    up_summed = lax.all_to_all(up_summed, "tensor", split_axis=1, concat_axis=3, tiled=True)
    stored_up, velocity_up = outer_step(
        master_up, moment_up, up_summed.reshape(rows_up, half_cols * tensors), replicas
    )
    stored_down, velocity_down = outer_step(master_down, moment_down, down_summed, replicas)
    norm_summed = lax.psum(trained_norm[0].astype(jnp.float32), "replica")
    stored_norm, velocity_norm = outer_step(master_norm, moment_norm, norm_summed, replicas)
    embed_own = master_embed[0]
    rows_embed = embed_own.shape[0]
    embed_terms = trained_embed[0].reshape(replicas, rows_embed, width).astype(jnp.float32)
    embed_summed = lax.psum_scatter(
        embed_terms.astype(jnp.bfloat16), "replica", scatter_dimension=0, tiled=True
    ).astype(jnp.float32)[0]
    coefficient = jnp.dot(
        embed_own - embed_summed / replicas, embed_basis, precision=lax.Precision.HIGHEST
    )
    velocity_rows = 0.5 * moment_embed[0] + coefficient
    stored_rows = embed_own - 0.7 * jnp.dot(
        coefficient + 0.5 * velocity_rows, embed_basis.T, precision=lax.Precision.HIGHEST
    )
    up_piece = lax.all_to_all(
        stored_up.astype(jnp.bfloat16), "tensor", split_axis=1, concat_axis=0, tiled=True
    )
    down_piece = stored_down[0].astype(jnp.bfloat16)
    recast_up, recast_down = (
        lax.all_gather(up_piece, ("replica", "shard"), axis=0, tiled=True),
        lax.all_gather(down_piece, ("replica", "shard"), axis=0, tiled=True),
    )
    recast_embed = lax.all_gather(stored_rows.astype(jnp.bfloat16), "replica", axis=0, tiled=True)
    return (
        recast_up,
        recast_down,
        recast_embed,
        stored_norm.astype(jnp.bfloat16),
        stored_up,
        velocity_up,
        stored_down,
        velocity_down,
        stored_rows[None],
        velocity_rows[None],
        stored_norm,
        velocity_norm,
    )


def solution(mesh):
    in_specs = (
        P("replica", None, "tensor"),
        P("replica", "tensor", None),
        P("replica", ("shard", "tensor"), None),
        P("replica", None, None),
        P(("replica", "shard", "tensor"), None),
        P(("replica", "shard", "tensor"), None),
        P("tensor", ("replica", "shard"), None),
        P("tensor", ("replica", "shard"), None),
        P(("shard", "tensor"), "replica", None),
        P(("shard", "tensor"), "replica", None),
        P(),
        P(),
        P(),
    )
    out_specs = (
        P(None, "tensor"),
        P("tensor", None),
        P(("shard", "tensor"), None),
        P(),
        P(("replica", "shard", "tensor"), None),
        P(("replica", "shard", "tensor"), None),
        P("tensor", ("replica", "shard"), None),
        P("tensor", ("replica", "shard"), None),
        P(("shard", "tensor"), "replica", None),
        P(("shard", "tensor"), "replica", None),
        P(),
        P(),
    )
    return jax.shard_map(body, mesh=mesh, in_specs=in_specs, out_specs=out_specs, check_vma=False)
```

profile of v0, /device:TPU:1, one launch (start us, length us, event | category | flops | bytes accessed | tf_op | source)
XLA Modules:
  0.0 376.6 jit_solution(8853071086595991756)
XLA Ops:
  7.2 0.0 copy-start
  7.2 0.0 copy-start.1
  7.2 0.0 copy-start.4
  7.2 0.0 reduce-scatter.6.cloned.1.call-start
  7.3 0.0 copy-start.12
  7.3 0.7 reduce-scatter.6.cloned.1.call-update
  7.9 0.0 copy-start.7
  8.0 0.0 copy-start.8
  8.0 0.0 all-reduce.3.cloned.1.call-start
  8.0 1.7 copy_bitcast_fusion
  9.7 0.0 copy-start.5
  9.7 0.0 copy-start.6
  9.7 0.0 all-reduce.3.cloned.1.call-update
  9.7 0.0 reduce-scatter.4.cloned.1.call-start
  9.8 0.0 copy-start.11
  9.8 1.7 dynamic-slice_bitcast_fusion
  11.5 0.0 copy-start.9
  11.5 0.0 copy-start.10
  11.5 0.0 reduce-scatter.4.cloned.1.call-update
  11.5 0.0 all-gather.7.cloned.1.call-start
  11.6 32.1 %reduce-scatter.6.cloned.1.call-done = bf16[1,256,1024]{2,1,0:T(8,128)(2,1)} async-done(((bf16[4,256,1024]{2,1,0:T(8,128)(2,1)}), bf16[1,256,1024]{2,1,0:T(8,128)(2,1)}) %reduce-scatter.6.cloned.1.call-update) | async-done | bytes 524304 | tf_op jit(solution)/shard_map/reduce_scatter | solution.py:64
  43.6 0.0 copy-done
  43.6 0.0 copy-done.1
  43.6 2.2 fusion.1
  45.8 0.0 copy-done.4
  45.8 2.2 fusion.16
  48.0 0.0 all-gather.7.cloned.1.call-update
  48.1 0.0 all-gather.5.cloned.1.call-start
  48.1 0.0 copy-done.12
  48.1 0.6 dynamic-slice
  48.7 37.3 %all-reduce.3.cloned.1.call-done = bf16[4,2,8,2048]{3,2,0,1:T(8,128)(2,1)} async-done(((bf16[4,2,8,2048]{3,2,0,1:T(8,128)(2,1)}), bf16[4,2,8,2048]{3,2,0,1:T(8,128)(2,1)}) %all-reduce.3.cloned.1.call-update) | async-done | bytes 262160
  86.0 1.5 dynamic-slice_convert_fusion
  87.5 8.6 %all_to_all.28 = f32[1,2,8,2048]{3,2,0,1:T(8,128)S(1)} all-to-all(f32[1,2,8,2048]{3,2,0,1:T(8,128)S(1)} %dynamic-slice_convert_fusion), channel_id=1, replica_groups=mesh['replica'=4,'shard'=16,'tensor'=2] {'tensor'}, dimensions={1} | all-to-all | bytes 262144 | tf_op jit(solution)/shard_map/all_to_all | solution.py:54
  96.1 0.0 copy-done.7
  96.1 0.0 copy-done.8
  96.1 0.7 fusion.15
  96.9 7.5 %all_to_all.29 = bf16[8,2,2048]{2,0,1:T(8,128)(2,1)} all-to-all(bf16[8,2,2048]{2,0,1:T(8,128)(2,1)S(1)} %bitcast.53), channel_id=1, replica_groups=mesh['replica'=4,'shard'=16,'tensor'=2] {'tensor'}, dimensions={1} | all-to-all | bytes 131072 | tf_op jit(solution)/shard_map/all_to_all | solution.py:74
  104.4 0.0 all-gather.5.cloned.1.call-update
  104.4 0.0 all-gather.9.cloned.1.call-start
  104.4 5.8 %reduce-scatter.4.cloned.1.call-done = bf16[1,32,1024]{2,1,0:T(8,128)(2,1)} async-done(((bf16[4,32,1024]{2,1,0:T(8,128)(2,1)}), bf16[1,32,1024]{2,1,0:T(8,128)(2,1)}) %reduce-scatter.4.cloned.1.call-update) | async-done | bytes 65552 | tf_op jit(solution)/shard_map/reduce_scatter | solution.py:47
  110.3 0.0 copy-done.5
  110.3 0.0 copy-done.6
  110.3 1.6 fusion.14
  111.9 0.0 all-gather.9.cloned.1.call-update
  111.9 0.0 copy-done.11
  111.9 6.9 %psum.7 = f32[2,1024]{1,0:T(2,128)S(1)} all-reduce(f32[2,1024]{1,0:T(2,128)S(1)} %bitcast_convert_fusion), channel_id=1, replica_groups=mesh['replica'=4,'shard'=16,'tensor'=2] {'replica'}, use_global_device_ids=true, to_apply=%region_3.4 | all-reduce | flops 2048 | bytes 16384 | tf_op jit(solution)/shard_map/psum | solution.py:59
  118.9 0.0 copy-done.9
  118.9 0.0 copy-done.10
  118.9 0.6 fusion.13
  119.5 0.6 fusion.8
  120.2 25.0 %all-gather.7.cloned.1.call-done = bf16[1024,1024]{1,0:T(8,128)(2,1)} async-done(((bf16[256,1024]{1,0:T(8,128)(2,1)}), bf16[1024,1024]{1,0:T(8,128)(2,1)}) %all-gather.7.cloned.1.call-update) | async-done | bytes 2097168 | tf_op jit(solution)/shard_map/all_gather | solution.py:82
  145.2 108.0 %all-gather.5.cloned.1.call-done = bf16[1024,2048]{1,0:T(8,128)(2,1)} async-done(((bf16[16,2048]{1,0:T(8,128)(2,1)}), bf16[1024,2048]{1,0:T(8,128)(2,1)}) %all-gather.5.cloned.1.call-update) | async-done | bytes 4194320 | tf_op jit(solution)/shard_map/all_gather | solution.py:79
  253.2 107.3 %all-gather.9.cloned.1.call-done = bf16[1,2048,1024]{2,1,0:T(8,128)(2,1)} async-done(((bf16[1,32,1024]{2,1,0:T(8,128)(2,1)}), bf16[1,2048,1024]{2,1,0:T(8,128)(2,1)}) %all-gather.9.cloned.1.call-update) | async-done | bytes 4194320 | tf_op jit(solution)/shard_map/all_gather | solution.py:80
  360.4 0.0 copy-start.2
  360.4 4.9 %copy.39 = bf16[1024,2048]{1,0:T(8,128)(2,1)} copy(bf16[1024,2048]{1,0:T(8,128)(2,1)} %all-gather.5.cloned.1.call-done) | data formatting | bytes 8388608
  365.4 0.0 copy-done.2
  365.4 0.0 copy-start.3
  365.4 2.1 copy.40
  367.5 1.0 copy-done.3
  368.5 1.3 copy.41
  (2 shorter events, 0.0 us)
Async XLA Ops:
  7.2 36.5 %copy-start = (f32[1024,64]{0,1:T(8,128)S(1)}, f32[1024,64]{0,1:T(8,128)}, u32[]{:S(2)}) copy-start(f32[1024,64]{0,1:T(8,128)} %param.25) | copy-start | bytes 786436
  7.2 36.5 %copy-start.1 = (f32[1,256,1024]{2,1,0:T(8,128)S(1)}, f32[1,256,1024]{2,1,0:T(8,128)}, u32[]{:S(2)}) copy-start(f32[1,256,1024]{2,1,0:T(8,128)} %param.21) | copy-start | bytes 3145732
  7.2 38.6 %copy-start.4 = (f32[1,256,64]{1,2,0:T(8,128)S(1)}, f32[1,256,64]{1,2,0:T(8,128)}, u32[]{:S(2)}) copy-start(f32[1,256,64]{1,2,0:T(8,128)} %param.22) | copy-start | bytes 196612
  7.2 36.4 %reduce-scatter.6.cloned.1.call-start = ((), (), s32[]{:S(2)}) async-start(), calls=%async_computation.6 | async-start | bytes 2621440 | tf_op jit(solution)/shard_map/reduce_scatter | solution.py:64
  7.3 40.9 %copy-start.12 = (u32[128]{0:T(128)S(1)}, u32[128]{0:T(128)}, u32[]{:S(2)}) copy-start(u32[128]{0:T(128)} %constant.47) | copy-start | bytes 1540
  7.9 88.2 %copy-start.7 = (f32[8,4096]{1,0:T(8,128)S(1)}, f32[8,4096]{1,0:T(8,128)}, u32[]{:S(2)}) copy-start(f32[8,4096]{1,0:T(8,128)} %param.17) | copy-start | bytes 393220
  8.0 88.2 %copy-start.8 = (f32[8,4096]{1,0:T(8,128)S(1)}, f32[8,4096]{1,0:T(8,128)}, u32[]{:S(2)}) copy-start(f32[8,4096]{1,0:T(8,128)} %param.18) | copy-start | bytes 393220
  8.0 78.0 %all-reduce.3.cloned.1.call-start = ((), (), s32[]{:S(2)}) async-start(), calls=%async_computation.9 | async-start | bytes 524288
  9.7 100.6 %copy-start.5 = (f32[1,32,1024]{2,1,0:T(8,128)S(1)}, f32[1,32,1024]{2,1,0:T(8,128)}, u32[]{:S(2)}) copy-start(f32[1,32,1024]{2,1,0:T(8,128)} %param.19) | copy-start | bytes 393220
  9.7 100.6 %copy-start.6 = (f32[1,32,1024]{2,1,0:T(8,128)S(1)}, f32[1,32,1024]{2,1,0:T(8,128)}, u32[]{:S(2)}) copy-start(f32[1,32,1024]{2,1,0:T(8,128)} %param.20) | copy-start | bytes 393220
  9.7 100.6 %reduce-scatter.4.cloned.1.call-start = ((), (), s32[]{:S(2)}) async-start(), calls=%async_computation.5 | async-start | bytes 327680 | tf_op jit(solution)/shard_map/reduce_scatter | solution.py:47
  9.8 102.1 %copy-start.11 = (bf16[1,2,1024]{2,1,0:T(2,128)(2,1)S(1)}, bf16[1,2,1024]{2,1,0:T(2,128)(2,1)}, u32[]{:S(2)}) copy-start(bf16[1,2,1024]{2,1,0:T(2,128)(2,1)} %param.16) | copy-start | bytes 12292
  11.5 107.4 %copy-start.9 = (f32[2,1024]{1,0:T(2,128)S(1)}, f32[2,1024]{1,0:T(2,128)}, u32[]{:S(2)}) copy-start(f32[2,1024]{1,0:T(2,128)} %param.23) | copy-start | bytes 24580
  11.5 107.4 %copy-start.10 = (f32[2,1024]{1,0:T(2,128)S(1)}, f32[2,1024]{1,0:T(2,128)}, u32[]{:S(2)}) copy-start(f32[2,1024]{1,0:T(2,128)} %param.24) | copy-start | bytes 24580
  11.5 133.6 %all-gather.7.cloned.1.call-start = ((), (), s32[]{:S(2)}) async-start(), calls=%async_computation.7 | async-start | bytes 2621440 | tf_op jit(solution)/shard_map/all_gather | solution.py:82
  48.1 205.1 %all-gather.5.cloned.1.call-start = ((), (), s32[]{:S(2)}) async-start(), calls=%async_computation.4 | async-start | bytes 4259840 | tf_op jit(solution)/shard_map/all_gather | solution.py:79
  104.4 256.0 %all-gather.9.cloned.1.call-start = ((), (), s32[]{:S(2)}) async-start(), calls=%async_computation.8 | async-start | bytes 4259840 | tf_op jit(solution)/shard_map/all_gather | solution.py:80
  360.4 4.9 %copy-start.2 = (bf16[1,2048,1024]{2,1,0:T(8,128)(2,1)S(1)}, bf16[1,2048,1024]{2,1,0:T(8,128)(2,1)}, u32[]{:S(2)}) copy-start(bf16[1,2048,1024]{2,1,0:T(8,128)(2,1)} %all-gather.9.cloned.1.call-done) | copy-start | bytes 12582916
  365.4 3.1 copy-start.3
Sparse Core Ops, SparseCore 0:
  10.4 33.1 reduce-scatter.5
  46.7 39.3 all-reduce.2
  89.0 21.2 reduce-scatter.3
  112.5 32.6 all-gather.6
  146.9 106.2 all-gather.4
  255.4 104.9 all-gather.8
where the time goes:
time: 377 us
  waiting for transfers between devices  316 us (84%)
  blocking collectives  23 us (6%)
  between operations  14.3 us (4%)
  local copies, waits for them, and re-layouts  13.4 us (4%)
  other arithmetic  5.09 us (1%)
  matrix products  4.38 us (1%)
    all_gather x1, waiting for transfers between devices, body(): lax.all_gather(up_piece, ('replica', 'shard'), axis=0, tiled=True)  108 us
    all_gather x1, waiting for transfers between devices, body(): lax.all_gather(down_piece, ('replica', 'shard'), axis=0, tiled=True)  107 us
    unnamed x7, waiting for transfers between devices  38.1 us
    reduce_scatter x1, waiting for transfers between devices, body(): lax.psum_scatter(embed_terms.astype(jnp.bfloat16), 'replica', scatter_dim...  32.1 us
    all_gather x1, waiting for transfers between devices, body(): lax.all_gather(stored_rows.astype(jnp.bfloat16), 'replica', axis=0, tiled...  25 us
    unnamed x30, local copies, waits for them, and re-layouts  10 us
    all_to_all x1, blocking collectives, body(): lax.all_to_all(up_summed, 'tensor', split_axis=1, concat_axis=3, tiled=True)  8.59 us
  transfers between devices with their start and end apart: 6, of which 6 were waited for; matrix products, arithmetic and copies ran while one was open for 4% of the time, Pallas kernels for 0%

commit v1 on v0

--- a/solution.py
+++ b/solution.py
@@ -51,7 +51,12 @@
             tiled=True,
         ).astype(jnp.float32),
     )
-    up_summed = lax.all_to_all(up_summed, "tensor", split_axis=1, concat_axis=3, tiled=True)
+    up_summed = jnp.concatenate(
+        lax.all_to_all(
+            jnp.stack(jnp.split(up_summed, lax.axis_size("tensor"), axis=1)), "tensor", 0, 0
+        ),
+        axis=3,
+    )
     stored_up, velocity_up = outer_step(
         master_up, moment_up, up_summed.reshape(rows_up, half_cols * tensors), replicas
     )

time: 377 us -> 356 us (0.944)
  waiting for transfers between devices: 316 us -> 295 us
    unnamed x7 -> x6, waiting for transfers between devices: 38.1 us -> 0.74 us
    reduce_scatter x0 -> x1, waiting for transfers between devices: none -> 21.8 us  [body(): lax.psum_scatter(up_own.astype(jnp.float32).astype(jnp.bfloat16), 'replic...]
    all_gather x1, waiting for transfers between devices: 25 us -> 8.26 us  [body(): lax.all_gather(stored_rows.astype(jnp.bfloat16), 'replica', axis=0, tiled...]
    reduce_scatter x1, waiting for transfers between devices: 5.85 us -> 16.7 us  [body(): lax.psum_scatter(down_own.astype(jnp.float32).astype(jnp.bfloat16), 'repl...]
    unnamed x30 -> x27, local copies, waits for them, and re-layouts: 10 us -> 9.42 us
  transfers between devices with their start and end apart: 6 -> 6, of which waited for: 6 -> 6; matrix products, arithmetic and copies ran while one was open for 4% -> 3% of each run, Pallas kernels for 0% -> 0%
where the time goes in v1:
time: 356 us; the launch traced here: 355 us
  waiting for transfers between devices  295 us (83%)
  blocking collectives  24.3 us (7%)
  between operations  14.3 us (4%)
  local copies, waits for them, and re-layouts  12.8 us (4%)
  other arithmetic  4.46 us (1%)
  matrix products  4.38 us (1%)
    all_gather x1, waiting for transfers between devices, body(): lax.all_gather(down_piece, ('replica', 'shard'), axis=0, tiled=True)  108 us
    all_gather x1, waiting for transfers between devices, body(): lax.all_gather(up_piece, ('replica', 'shard'), axis=0, tiled=True)  107 us
    reduce_scatter x1, waiting for transfers between devices, body(): lax.psum_scatter(embed_terms.astype(jnp.bfloat16), 'replica', scatter_dim...  32.1 us
    reduce_scatter x1, waiting for transfers between devices, body(): lax.psum_scatter(up_own.astype(jnp.float32).astype(jnp.bfloat16), 'replic...  21.8 us
    reduce_scatter x1, waiting for transfers between devices, body(): lax.psum_scatter(down_own.astype(jnp.float32).astype(jnp.bfloat16), 'repl...  16.7 us
    unnamed x27, local copies, waits for them, and re-layouts  9.42 us
    all_to_all x1, blocking collectives, body(): lax.all_to_all(jnp.stack(jnp.split(up_summed, lax.axis_size('tensor'), ax...  8.6 us
    all_gather x1, waiting for transfers between devices, body(): lax.all_gather(stored_rows.astype(jnp.bfloat16), 'replica', axis=0, tiled...  8.26 us
  transfers between devices with their start and end apart: 6, of which 6 were waited for; matrix products, arithmetic and copies ran while one was open for 3% of the time, Pallas kernels for 0%

profile of v1, /device:TPU:1, one launch (start us, length us, event | category | flops | bytes accessed | tf_op | source)
XLA Modules:
  0.0 355.1 jit_solution(1200229312679613573)
XLA Ops:
  7.2 0.0 copy-start
  7.2 0.0 copy-start.1
  7.2 0.0 copy-start.4
  7.2 0.0 reduce-scatter.8.cloned.1.call-start
  7.3 0.0 copy-start.5
  7.3 0.0 copy-start.6
  7.3 0.7 reduce-scatter.8.cloned.1.call-update
  7.9 0.0 reduce-scatter.6.cloned.1.call-start
  8.0 1.7 dynamic-slice_bitcast_fusion
  9.7 0.0 copy-start.7
  9.7 0.0 copy-start.8
  9.7 0.0 reduce-scatter.6.cloned.1.call-update
  9.7 0.0 reduce-scatter.4.cloned.1.call-start
  9.8 1.7 dynamic-slice_bitcast_fusion.1
  11.5 0.0 reduce-scatter.4.cloned.1.call-update
  11.5 0.0 copy-start.11
  11.5 0.0 copy-start.9
  11.5 0.0 copy-start.10
  11.5 0.0 all-gather.7.cloned.1.call-start
  11.6 32.1 %reduce-scatter.8.cloned.1.call-done = bf16[1,256,1024]{2,1,0:T(8,128)(2,1)} async-done(((bf16[4,256,1024]{2,1,0:T(8,128)(2,1)}), bf16[1,256,1024]{2,1,0:T(8,128)(2,1)}) %reduce-scatter.8.cloned.1.call-update) | async-done | bytes 524304 | tf_op jit(solution)/shard_map/reduce_scatter | solution.py:69
  43.6 0.0 copy-done
  43.6 0.0 copy-done.1
  43.6 2.2 fusion.1
  45.8 0.0 copy-done.4
  45.8 2.2 fusion.16
  48.0 0.0 all-gather.7.cloned.1.call-update
  48.1 0.0 all-gather.9.cloned.1.call-start
  48.1 16.7 %reduce-scatter.6.cloned.1.call-done = bf16[1,32,1024]{2,1,0:T(8,128)(2,1)} async-done(((bf16[4,32,1024]{2,1,0:T(8,128)(2,1)}), bf16[1,32,1024]{2,1,0:T(8,128)(2,1)}) %reduce-scatter.6.cloned.1.call-update) | async-done | bytes 65552 | tf_op jit(solution)/shard_map/reduce_scatter | solution.py:47
  64.9 0.0 copy-done.5
  64.9 0.0 copy-done.6
  64.9 1.6 fusion.14
  66.5 0.0 all-gather.9.cloned.1.call-update
  66.5 0.0 all-gather.5.cloned.1.call-start
  66.5 21.8 %reduce-scatter.4.cloned.1.call-done = bf16[1,2,8,2048]{3,2,1,0:T(8,128)(2,1)} async-done(((bf16[4,2,8,2048]{3,2,1,0:T(8,128)(2,1)}), bf16[1,2,8,2048]{3,2,1,0:T(8,128)(2,1)}) %reduce-scatter.4.cloned.1.call-update) | async-done | bytes 65552 | tf_op jit(solution)/shard_map/reduce_scatter | solution.py:41
  88.3 0.8 convert_element_type.36
  89.2 8.6 %all_to_all.24 = f32[2,1,1,8,2048]{4,3,2,1,0:T(8,128)S(1)} all-to-all(f32[2,1,1,8,2048]{4,3,2,1,0:T(8,128)S(1)} %pad_maximum_fusion), channel_id=1, replica_groups=mesh['replica'=4,'shard'=16,'tensor'=2] {'tensor'}, dimensions={0} | all-to-all | bytes 262144 | tf_op jit(solution)/shard_map/all_to_all | solution.py:55
  97.8 0.0 copy-done.7
  97.8 0.0 copy-done.8
  97.8 0.7 fusion.15
  98.6 7.5 %all_to_all.25 = bf16[8,2,2048]{2,0,1:T(8,128)(2,1)} all-to-all(bf16[8,2,2048]{2,0,1:T(8,128)(2,1)S(1)} %bitcast.54), channel_id=1, replica_groups=mesh['replica'=4,'shard'=16,'tensor'=2] {'tensor'}, dimensions={1} | all-to-all | bytes 131072 | tf_op jit(solution)/shard_map/all_to_all | solution.py:79
  106.0 0.0 all-gather.5.cloned.1.call-update
  106.1 0.0 copy-done.11
  106.1 8.2 %psum.7 = f32[2,1024]{1,0:T(2,128)S(1)} all-reduce(f32[2,1024]{1,0:T(2,128)S(1)} %bitcast_convert_fusion), channel_id=1, replica_groups=mesh['replica'=4,'shard'=16,'tensor'=2] {'replica'}, use_global_device_ids=true, to_apply=%region_3.4 | all-reduce | flops 2048 | bytes 16384 | tf_op jit(solution)/shard_map/psum | solution.py:64
  114.3 0.0 copy-done.9
  114.3 0.0 copy-done.10
  114.3 0.6 fusion.13
  114.9 0.6 fusion.8
  115.5 8.3 %all-gather.7.cloned.1.call-done = bf16[1024,1024]{1,0:T(8,128)(2,1)} async-done(((bf16[256,1024]{1,0:T(8,128)(2,1)}), bf16[1024,1024]{1,0:T(8,128)(2,1)}) %all-gather.7.cloned.1.call-update) | async-done | bytes 2097168 | tf_op jit(solution)/shard_map/all_gather | solution.py:87
  123.8 108.4 %all-gather.9.cloned.1.call-done = bf16[1,2048,1024]{2,1,0:T(8,128)(2,1)} async-done(((bf16[1,32,1024]{2,1,0:T(8,128)(2,1)}), bf16[1,2048,1024]{2,1,0:T(8,128)(2,1)}) %all-gather.9.cloned.1.call-update) | async-done | bytes 4194320 | tf_op jit(solution)/shard_map/all_gather | solution.py:85
  232.2 106.7 %all-gather.5.cloned.1.call-done = bf16[1024,2048]{1,0:T(8,128)(2,1)} async-done(((bf16[16,2048]{1,0:T(8,128)(2,1)}), bf16[1024,2048]{1,0:T(8,128)(2,1)}) %all-gather.5.cloned.1.call-update) | async-done | bytes 4194320 | tf_op jit(solution)/shard_map/all_gather | solution.py:84
  338.9 0.0 copy-start.2
  338.9 4.9 %copy.34 = bf16[1024,2048]{1,0:T(8,128)(2,1)} copy(bf16[1024,2048]{1,0:T(8,128)(2,1)} %all-gather.5.cloned.1.call-done) | data formatting | bytes 8388608
  343.8 0.0 copy-done.2
  343.8 0.0 copy-start.3
  343.8 2.1 copy.35
  346.0 1.0 copy-done.3
  346.9 1.3 copy.36
  (4 shorter events, 0.0 us)
Async XLA Ops:
  7.2 36.5 %copy-start = (f32[1024,64]{0,1:T(8,128)S(1)}, f32[1024,64]{0,1:T(8,128)}, u32[]{:S(2)}) copy-start(f32[1024,64]{0,1:T(8,128)} %param.25) | copy-start | bytes 786436
  7.2 36.5 %copy-start.1 = (f32[1,256,1024]{2,1,0:T(8,128)S(1)}, f32[1,256,1024]{2,1,0:T(8,128)}, u32[]{:S(2)}) copy-start(f32[1,256,1024]{2,1,0:T(8,128)} %param.21) | copy-start | bytes 3145732
  7.2 38.6 %copy-start.4 = (f32[1,256,64]{1,2,0:T(8,128)S(1)}, f32[1,256,64]{1,2,0:T(8,128)}, u32[]{:S(2)}) copy-start(f32[1,256,64]{1,2,0:T(8,128)} %param.22) | copy-start | bytes 196612
  7.2 36.4 %reduce-scatter.8.cloned.1.call-start = ((), (), s32[]{:S(2)}) async-start(), calls=%async_computation.8 | async-start | bytes 2621440 | tf_op jit(solution)/shard_map/reduce_scatter | solution.py:69
  7.3 57.6 %copy-start.5 = (f32[1,32,1024]{2,1,0:T(8,128)S(1)}, f32[1,32,1024]{2,1,0:T(8,128)}, u32[]{:S(2)}) copy-start(f32[1,32,1024]{2,1,0:T(8,128)} %param.19) | copy-start | bytes 393220
  7.3 57.6 %copy-start.6 = (f32[1,32,1024]{2,1,0:T(8,128)S(1)}, f32[1,32,1024]{2,1,0:T(8,128)}, u32[]{:S(2)}) copy-start(f32[1,32,1024]{2,1,0:T(8,128)} %param.20) | copy-start | bytes 393220
  7.9 56.9 %reduce-scatter.6.cloned.1.call-start = ((), (), s32[]{:S(2)}) async-start(), calls=%async_computation.7 | async-start | bytes 327680 | tf_op jit(solution)/shard_map/reduce_scatter | solution.py:47
  9.7 88.1 %copy-start.7 = (f32[8,4096]{1,0:T(8,128)S(1)}, f32[8,4096]{1,0:T(8,128)}, u32[]{:S(2)}) copy-start(f32[8,4096]{1,0:T(8,128)} %param.17) | copy-start | bytes 393220
  9.7 88.1 %copy-start.8 = (f32[8,4096]{1,0:T(8,128)S(1)}, f32[8,4096]{1,0:T(8,128)}, u32[]{:S(2)}) copy-start(f32[8,4096]{1,0:T(8,128)} %param.18) | copy-start | bytes 393220
  9.7 78.6 %reduce-scatter.4.cloned.1.call-start = ((), (), s32[]{:S(2)}) async-start(), calls=%async_computation.5 | async-start | bytes 327680 | tf_op jit(solution)/shard_map/reduce_scatter | solution.py:41
  11.5 94.6 %copy-start.11 = (bf16[1,2,1024]{2,1,0:T(2,128)(2,1)S(1)}, bf16[1,2,1024]{2,1,0:T(2,128)(2,1)}, u32[]{:S(2)}) copy-start(bf16[1,2,1024]{2,1,0:T(2,128)(2,1)} %param.16) | copy-start | bytes 12292
  11.5 102.8 %copy-start.9 = (f32[2,1024]{1,0:T(2,128)S(1)}, f32[2,1024]{1,0:T(2,128)}, u32[]{:S(2)}) copy-start(f32[2,1024]{1,0:T(2,128)} %param.23) | copy-start | bytes 24580
  11.5 102.8 %copy-start.10 = (f32[2,1024]{1,0:T(2,128)S(1)}, f32[2,1024]{1,0:T(2,128)}, u32[]{:S(2)}) copy-start(f32[2,1024]{1,0:T(2,128)} %param.24) | copy-start | bytes 24580
  11.5 112.3 %all-gather.7.cloned.1.call-start = ((), (), s32[]{:S(2)}) async-start(), calls=%async_computation.9 | async-start | bytes 2621440 | tf_op jit(solution)/shard_map/all_gather | solution.py:87
  48.1 184.1 %all-gather.9.cloned.1.call-start = ((), (), s32[]{:S(2)}) async-start(), calls=%async_computation.10 | async-start | bytes 4259840 | tf_op jit(solution)/shard_map/all_gather | solution.py:85
  66.5 272.4 %all-gather.5.cloned.1.call-start = ((), (), s32[]{:S(2)}) async-start(), calls=%async_computation.6 | async-start | bytes 4259840 | tf_op jit(solution)/shard_map/all_gather | solution.py:84
  338.9 4.9 %copy-start.2 = (bf16[1,2048,1024]{2,1,0:T(8,128)(2,1)S(1)}, bf16[1,2048,1024]{2,1,0:T(8,128)(2,1)}, u32[]{:S(2)}) copy-start(bf16[1,2048,1024]{2,1,0:T(8,128)(2,1)} %all-gather.9.cloned.1.call-done) | copy-start | bytes 12582916
  343.8 3.1 copy-start.3
Sparse Core Ops, SparseCore 0:
  10.4 33.1 reduce-scatter.7
  46.7 18.1 reduce-scatter.5
  67.8 20.4 reduce-scatter.3
  90.5 33.2 all-gather.6
  126.1 106.0 all-gather.8
  233.9 104.9 all-gather.4
